TPU v7x, 32 devices: a whole 2x2x4 slice. The times are simulated.
32 devices in a mesh: fsdp: 2 (over x), ctx: 4 (over y, core), tp: 4 (over z).
Axes of the slice: x: 2, y: 2, z: 4, core: 2. Of those that a mesh axis runs over, the one named last changes fastest.
Arguments:
- tokens: bfloat16 [8, 512, 768], P(('fsdp', 'tp'), 'ctx'), may hold values from -6 to 6
- seg_ids: int32 [8, 512], P(('fsdp', 'tp')), may hold values from 0 to 2, never falling along the last dimension, each value on 1 to 384 neighbouring positions
- routes: int32 [8, 512, 2], P(('fsdp', 'tp'), 'ctx'), may hold values from 0 to 3, all different within a row; in each aligned block of 128 rows (0 to 127, 128 to 255, ..., all dimensions but the last counted through in order) at most 80 rows name the same one
- norm_attn: bfloat16 [768], P('fsdp'), may hold values from 0.5 to 1.5
- weight_qkv: bfloat16 [768, 2304], P('fsdp'), may hold values from -0.21875 to 0.21875
- weight_proj: bfloat16 [768, 768], P(None, 'fsdp'), may hold values from -0.875 to 0.875
- rel_table: float32 [12, 32], replicated, may hold values from -4 to 4
- norm_ffn: bfloat16 [768], P('fsdp'), may hold values from 0.5 to 1.5
- weight_router: bfloat16 [768, 4], P('fsdp'), may hold values from -0.21875 to 0.21875
- expert_up: bfloat16 [4, 768, 3072], P(None, 'fsdp', ('ctx', 'tp')), may hold values from -0.21875 to 0.21875
- expert_down: bfloat16 [4, 3072, 768], P(None, ('ctx', 'tp'), 'fsdp'), may hold values from -0.109375 to 0.109375
- cotangent: bfloat16 [8, 512, 768], P(('fsdp', 'tp'), 'ctx'), may hold values from -6 to 6
Outputs:
- output: bfloat16 [8, 512, 768], P(('fsdp', 'tp'), 'ctx')
- grad_tokens: float32 [8, 512, 768], P(('fsdp', 'tp'), 'ctx')
- grad_norm_attn: float32 [768], P('fsdp')
- grad_weight_qkv: float32 [768, 2304], P('fsdp')
- grad_weight_proj: float32 [768, 768], P(None, 'fsdp')
- grad_rel_table: float32 [12, 32], replicated
- grad_norm_ffn: float32 [768], P('fsdp')
- grad_weight_router: float32 [768, 4], P('fsdp')
- grad_expert_up: float32 [4, 768, 3072], P(None, 'fsdp', ('ctx', 'tp'))
- grad_expert_down: float32 [4, 3072, 768], P(None, ('ctx', 'tp'), 'fsdp')
Inputs may be any that keep to these rules, and one draw needn't show every extreme that they name: `seg_ids`: each group's 512 positions fall into at most 3 sequences whose numbers never fall along the positions; the longest has exactly 384 positions. `routes`: each token names two different experts. In each aligned block of 128 rows (the rows of one device) no expert is named more than 80 times, and in every draw some expert is named exactly 80 times in some block.
All inputs are finite; a program needn't handle non-finite values.
Results may differ from a plain program's by a relative error of at most 0.012.
Values may be sent and summed in bfloat16 or wider, within the bound.
A program may use at most 192 MiB of HBM per device.

v0:
```python
import jax
import jax.numpy as jnp
import numpy as np
from jax import lax
from jax.sharding import PartitionSpec as P

BUCKETS = 32
MAX_DISTANCE = 128
MOST = 80


EPSILON = 1e-06
MASK_FILL = -1e30


def bucket_bounds(buckets, far_reach):
    exact_count = buckets // 2
    bounds = []
    for number in range(1, buckets):
        if number <= exact_count:
            bounds.append(number)
        else:
            exponent = (number - exact_count) / (buckets - exact_count)
            bounds.append(int(np.ceil(exact_count * (far_reach / exact_count) ** exponent)))
    return np.array(bounds, dtype=np.int32)


def bucket_onehot(length):
    bounds = jnp.asarray(bucket_bounds(BUCKETS, MAX_DISTANCE))
    distance = jnp.arange(length, dtype=jnp.int32)
    which_bucket = jnp.sum((distance[:, None] >= bounds[None, :]).astype(jnp.int32), axis=1)
    return (which_bucket[:, None] == jnp.arange(BUCKETS, dtype=jnp.int32)[None, :]).astype(
        jnp.float32
    )


def spread_diagonals(vectors):
    heads_here, length = vectors.shape
    padded = jnp.concatenate([vectors[:, ::-1], jnp.zeros_like(vectors)], axis=1)
    repeated = jnp.tile(padded, (1, length))
    window = repeated[:, length - 1 : length - 1 + length * (2 * length - 1)]
    return window.reshape(heads_here, length, 2 * length - 1)[:, :, :length]


def slot_tables(route_ids, experts, capacity):
    flat_ids = route_ids.reshape(-1)
    assignments = flat_ids.shape[0]
    member = (flat_ids[:, None] == jnp.arange(experts, dtype=jnp.int32)[None, :]).astype(jnp.int32)
    before = jnp.cumsum(member, axis=0) - member
    slot_index = jnp.sum(before * member, axis=1)
    position = slot_index * experts + flat_ids
    filler = (
        jnp.full((capacity * experts,), assignments, jnp.int32)
        .at[position]
        .set(jnp.arange(assignments, dtype=jnp.int32))
    )
    return (position, filler)


def rms_scale(values):
    return lax.rsqrt(jnp.mean(values * values, axis=-1, keepdims=True) + EPSILON)


def local(
    tokens,
    seg_ids,
    routes,
    norm_attn,
    weight_qkv,
    weight_proj,
    rel_table,
    norm_ffn,
    weight_router,
    expert_up,
    expert_down,
    cotangent,
):
    row_count = tokens.shape[1]
    model_width = tokens.shape[2]
    head_count = rel_table.shape[0]
    head_size = model_width // head_count
    heads_here = head_count // lax.axis_size("ctx")
    expert_count = expert_up.shape[0]
    length = seg_ids.shape[1]
    score_scale = head_size ** (-0.5)
    ctx_index = lax.axis_index("ctx")
    head_width = heads_here * head_size
    gathered = (
        lax.all_gather(norm_attn, "fsdp", axis=0, tiled=True),
        lax.all_gather(weight_qkv, "fsdp", axis=0, tiled=True),
        lax.all_gather(weight_proj, "fsdp", axis=1, tiled=True),
        lax.all_gather(weight_router, "fsdp", axis=0, tiled=True),
        lax.all_gather(norm_ffn, "fsdp", axis=0, tiled=True),
        lax.all_gather(expert_up, "fsdp", axis=1, tiled=True),
        lax.all_gather(expert_down, "fsdp", axis=2, tiled=True),
    )
    gain_one, qkv_full, proj_full, router_full, gain_two, up_full, down_full = gathered
    inputs = tokens[0].astype(jnp.float32)
    scale_one = rms_scale(inputs)
    normed_one = (inputs * scale_one * gain_one.astype(jnp.float32)).astype(jnp.bfloat16)
    projected = jnp.dot(normed_one, qkv_full, preferred_element_type=jnp.float32).astype(
        jnp.bfloat16
    )
    by_head = lax.all_to_all(
        projected.reshape(row_count, 3, head_count, head_size),
        "ctx",
        split_axis=2,
        concat_axis=0,
        tiled=True,
    )
    query_rows = by_head[:, 0]
    key_rows = by_head[:, 1]
    value_rows = by_head[:, 2]
    table_here = lax.dynamic_slice_in_dim(rel_table, ctx_index * heads_here, heads_here, 0)
    onehot = bucket_onehot(length)
    bias_vector = jnp.dot(table_here, onehot.T, precision=lax.Precision.HIGHEST)
    bias_matrix = spread_diagonals(bias_vector)
    positions = jnp.arange(length, dtype=jnp.int32)
    segment = seg_ids[0]
    allowed = (segment[:, None] == segment[None, :]) & (positions[:, None] >= positions[None, :])
    block_count = length // length
    query_blocks = query_rows.reshape(block_count, length, heads_here, head_size)
    bias_blocks = jnp.moveaxis(bias_matrix.reshape(heads_here, block_count, length, length), 1, 0)
    mask_blocks = allowed.reshape(block_count, length, length)

    def block_scores(query_block, bias_block, mask_block):
        products = jnp.einsum(
            "qhd,khd->hqk", query_block, key_rows, preferred_element_type=jnp.float32
        )
        return jnp.where(mask_block[None], products * score_scale + bias_block, MASK_FILL)

    def forward_block(pieces):
        query_block, bias_block, mask_block = pieces
        scores = block_scores(query_block, bias_block, mask_block)
        row_peak = jnp.max(scores, axis=-1, keepdims=True)
        weights = jnp.exp(scores - row_peak)
        row_total = jnp.sum(weights, axis=-1, keepdims=True)
        low_probs = (weights / row_total).astype(jnp.bfloat16)
        attended = jnp.einsum(
            "hqk,khd->qhd", low_probs, value_rows, preferred_element_type=jnp.float32
        ).astype(jnp.bfloat16)
        return (attended, (row_peak + jnp.log(row_total))[..., 0])

    attended_blocks, log_totals = lax.map(forward_block, (query_blocks, bias_blocks, mask_blocks))
    attended_heads = attended_blocks.reshape(length, heads_here, head_size)
    back_tokens = lax.all_to_all(attended_heads, "ctx", split_axis=0, concat_axis=1, tiled=True)
    mixed_heads = back_tokens.reshape(row_count, model_width)
    attention = jnp.dot(mixed_heads, proj_full, preferred_element_type=jnp.float32)
    middle = inputs + attention
    scale_two = rms_scale(middle)
    normed_two = (middle * scale_two * gain_two.astype(jnp.float32)).astype(jnp.bfloat16)
    logits = jnp.dot(normed_two, router_full, preferred_element_type=jnp.float32)
    route_ids = routes[0]
    choose = (
        route_ids[:, :, None] == jnp.arange(expert_count, dtype=jnp.int32)[None, None, :]
    ).astype(jnp.float32)
    picked = jnp.sum(choose * logits[:, None, :], axis=2)
    gate_raw = jnp.exp(picked - jnp.max(picked, axis=1, keepdims=True))
    gate_weights = gate_raw / jnp.sum(gate_raw, axis=1, keepdims=True)
    position, filler = slot_tables(route_ids, expert_count, MOST)
    padded_rows = jnp.concatenate([normed_two, jnp.zeros((1, model_width), jnp.bfloat16)], axis=0)
    dispatched = padded_rows[filler // 2].reshape(MOST, expert_count, model_width)
    arrived = lax.all_gather(dispatched, ("ctx", "tp"), axis=0, tiled=True)
    pre_act = jnp.einsum("sed,edf->sef", arrived, up_full, preferred_element_type=jnp.float32)
    activated = jax.nn.gelu(pre_act).astype(jnp.bfloat16)
    row_block = activated
    expert_result = lax.psum_scatter(
        jnp.einsum("sef,efd->sed", row_block, down_full, preferred_element_type=jnp.float32),
        ("ctx", "tp"),
        scatter_dimension=0,
        tiled=True,
    )
    per_choice = expert_result.reshape(MOST * expert_count, model_width)[position].reshape(
        row_count, 2, model_width
    )
    result = middle + jnp.sum(gate_weights[:, :, None] * per_choice, axis=1)
    output = result.astype(jnp.bfloat16)[None]
    again = (
        lax.all_gather(norm_attn, "fsdp", axis=0, tiled=True),
        lax.all_gather(weight_qkv, "fsdp", axis=0, tiled=True),
        lax.all_gather(weight_proj, "fsdp", axis=1, tiled=True),
        lax.all_gather(weight_router, "fsdp", axis=0, tiled=True),
        lax.all_gather(norm_ffn, "fsdp", axis=0, tiled=True),
        lax.all_gather(expert_up, "fsdp", axis=1, tiled=True),
        lax.all_gather(expert_down, "fsdp", axis=2, tiled=True),
    )
    gain_first, qkv_again, proj_again, router_again, gain_second, up_again, down_again = again
    grad_out = cotangent[0].astype(jnp.float32)
    gate_dots = jnp.sum(grad_out[:, None, :] * per_choice, axis=2)
    grad_pick = gate_weights * (
        gate_dots - jnp.sum(gate_weights * gate_dots, axis=1, keepdims=True)
    )
    grad_logits = jnp.sum(grad_pick[:, :, None] * choose, axis=1)
    grad_choice = (
        (gate_weights[:, :, None] * grad_out[:, None, :])
        .astype(jnp.bfloat16)
        .reshape(2 * row_count, model_width)
    )
    padded_grads = jnp.concatenate([grad_choice, jnp.zeros((1, model_width), jnp.bfloat16)], axis=0)
    grad_slots = padded_grads[filler].reshape(MOST, expert_count, model_width)
    grad_arrived = lax.all_gather(grad_slots, ("ctx", "tp"), axis=0, tiled=True)
    grad_act = jnp.einsum(
        "sed,efd->sef", grad_arrived, down_again, preferred_element_type=jnp.float32
    )
    grad_down = jnp.einsum(
        "sef,sed->efd", activated, grad_arrived, preferred_element_type=jnp.float32
    )
    gelu_back = jax.vjp(jax.nn.gelu, pre_act)[1]
    grad_pre = gelu_back(grad_act)[0].astype(jnp.bfloat16)
    grad_up = jnp.einsum("sed,sef->edf", arrived, grad_pre, preferred_element_type=jnp.float32)
    row_block = grad_pre
    grad_dispatched = lax.psum_scatter(
        jnp.einsum("sef,edf->sed", row_block, up_again, preferred_element_type=jnp.float32),
        ("ctx", "tp"),
        scatter_dimension=0,
        tiled=True,
    )
    grad_normed_two = jnp.sum(
        grad_dispatched.reshape(MOST * expert_count, model_width)[position].reshape(
            row_count, 2, model_width
        ),
        axis=1,
    )
    router_float = router_again.astype(jnp.float32)
    grad_normed_two = grad_normed_two + jnp.dot(
        grad_logits, router_float.T, precision=lax.Precision.HIGHEST
    )
    grad_router = jnp.dot(
        normed_two.astype(jnp.float32).T, grad_logits, precision=lax.Precision.HIGHEST
    )
    weighted_two = grad_normed_two * gain_second.astype(jnp.float32)
    grad_gain_two = jnp.sum(grad_normed_two * middle * scale_two, axis=0)
    grad_middle = (
        grad_out
        + scale_two * weighted_two
        - middle * scale_two**3 * jnp.mean(weighted_two * middle, axis=1, keepdims=True)
    )
    grad_middle_low = grad_middle.astype(jnp.bfloat16)
    normed_group, grad_mid_group = (
        lax.all_gather(normed_one, "ctx", axis=0, tiled=True),
        lax.all_gather(grad_middle_low, "ctx", axis=0, tiled=True),
    )
    proj_rows = lax.dynamic_slice_in_dim(proj_again, ctx_index * head_width, head_width, 0)
    grad_attended = jnp.einsum(
        "te,de->td", grad_mid_group, proj_rows, preferred_element_type=jnp.float32
    ).astype(jnp.bfloat16)
    grad_proj_part = jnp.einsum(
        "td,te->de",
        attended_heads.reshape(length, head_width),
        grad_mid_group,
        preferred_element_type=jnp.float32,
    )
    grad_blocks = grad_attended.reshape(block_count, length, heads_here, head_size)

    def backward_block(running, pieces):
        key_sum, value_sum = running
        query_block, bias_block, mask_block, log_block, grad_block = pieces
        scores = block_scores(query_block, bias_block, mask_block)
        probs_float = jnp.exp(scores - log_block[..., None])
        low_probs = probs_float.astype(jnp.bfloat16)
        value_term = jnp.einsum(
            "hqk,qhd->khd", low_probs, grad_block, preferred_element_type=jnp.float32
        )
        grad_probs = jnp.einsum(
            "qhd,khd->hqk", grad_block, value_rows, preferred_element_type=jnp.float32
        )
        grad_scores = (
            probs_float * (grad_probs - jnp.sum(probs_float * grad_probs, axis=-1, keepdims=True))
        ).astype(jnp.bfloat16)
        query_term = (
            jnp.einsum("hqk,khd->qhd", grad_scores, key_rows, preferred_element_type=jnp.float32)
            * score_scale
        ).astype(jnp.bfloat16)
        key_term = (
            jnp.einsum("hqk,qhd->khd", grad_scores, query_block, preferred_element_type=jnp.float32)
            * score_scale
        )
        return ((key_sum + key_term, value_sum + value_term), (query_term, grad_scores))

    zero_rows = jnp.zeros((length, heads_here, head_size), jnp.float32)
    sums_kv, per_block = lax.scan(
        backward_block,
        (zero_rows, zero_rows),
        (query_blocks, bias_blocks, mask_blocks, log_totals, grad_blocks),
    )
    query_grads, score_grads = per_block
    grad_qkv_heads = jnp.stack(
        [
            query_grads.reshape(length, heads_here, head_size),
            sums_kv[0].astype(jnp.bfloat16),
            sums_kv[1].astype(jnp.bfloat16),
        ],
        axis=1,
    )
    grad_qkv_part = jnp.einsum(
        "td,tshk->dshk", normed_group, grad_qkv_heads, preferred_element_type=jnp.float32
    )
    grad_projected = lax.all_to_all(
        grad_qkv_heads, "ctx", split_axis=0, concat_axis=2, tiled=True
    ).reshape(row_count, 3 * model_width)
    score_matrix = (
        jnp.moveaxis(score_grads, 0, 1).reshape(heads_here, length, length).astype(jnp.float32)
    )
    spread_back = jax.vjp(spread_diagonals, bias_vector)[1]
    grad_vector = spread_back(score_matrix)[0]
    grad_table_here = jnp.dot(grad_vector, onehot, precision=lax.Precision.HIGHEST)
    table_term = lax.dynamic_update_slice_in_dim(
        jnp.zeros((head_count, BUCKETS), jnp.float32), grad_table_here, ctx_index * heads_here, 0
    )
    grad_normed_one = jnp.einsum(
        "te,de->td", grad_projected, qkv_again, preferred_element_type=jnp.float32
    )
    weighted_one = grad_normed_one * gain_first.astype(jnp.float32)
    grad_gain_one = jnp.sum(grad_normed_one * inputs * scale_one, axis=0)
    grad_tokens = (
        grad_middle
        + scale_one * weighted_one
        - inputs * scale_one**3 * jnp.mean(weighted_one * inputs, axis=1, keepdims=True)
    )
    shares = (
        lax.psum_scatter(grad_gain_one, "fsdp", scatter_dimension=0, tiled=True),
        lax.psum_scatter(grad_qkv_part, "fsdp", scatter_dimension=0, tiled=True),
        lax.psum_scatter(grad_proj_part, "fsdp", scatter_dimension=1, tiled=True),
        lax.psum_scatter(grad_router, "fsdp", scatter_dimension=0, tiled=True),
        lax.psum_scatter(grad_gain_two, "fsdp", scatter_dimension=0, tiled=True),
        lax.psum_scatter(grad_up, "fsdp", scatter_dimension=1, tiled=True),
        lax.psum_scatter(grad_down, "fsdp", scatter_dimension=2, tiled=True),
    )
    qkv_share = shares[1]
    own_rows = qkv_share.shape[0]
    qkv_placed = lax.dynamic_update_slice_in_dim(
        jnp.zeros((own_rows, 3, head_count, head_size), jnp.float32),
        qkv_share,
        ctx_index * heads_here,
        2,
    ).reshape(own_rows, 3 * model_width)
    proj_share = shares[2]
    proj_placed = lax.dynamic_update_slice_in_dim(
        jnp.zeros((model_width, proj_share.shape[1]), jnp.float32),
        proj_share,
        ctx_index * head_width,
        0,
    )
    summed = lax.psum((shares[0], qkv_placed, proj_placed, shares[3], shares[4]), ("ctx", "tp"))
    table_grad = lax.psum(table_term, ("fsdp", "ctx", "tp"))
    return (
        output,
        grad_tokens[None],
        summed[0],
        summed[1],
        summed[2],
        table_grad,
        summed[4],
        summed[3],
        shares[5],
        shares[6],
    )


def solution(mesh):
    in_specs = (
        P(("fsdp", "tp"), "ctx", None),
        P(("fsdp", "tp"), None),
        P(("fsdp", "tp"), "ctx", None),
        P("fsdp"),
        P("fsdp", None),
        P(None, "fsdp"),
        P(),
        P("fsdp"),
        P("fsdp", None),
        P(None, "fsdp", ("ctx", "tp")),
        P(None, ("ctx", "tp"), "fsdp"),
        P(("fsdp", "tp"), "ctx", None),
    )
    out_specs = (
        P(("fsdp", "tp"), "ctx", None),
        P(("fsdp", "tp"), "ctx", None),
        P("fsdp"),
        P("fsdp", None),
        P(None, "fsdp"),
        P(),
        P("fsdp"),
        P("fsdp", None),
        P(None, "fsdp", ("ctx", "tp")),
        P(None, ("ctx", "tp"), "fsdp"),
    )
    return jax.shard_map(local, mesh=mesh, in_specs=in_specs, out_specs=out_specs, check_vma=False)
```

profile of v0, /device:TPU:0, one launch (start us, length us, event | category | flops | bytes accessed | tf_op | source)
XLA Modules:
  0.0 897.2 jit_solution(6429418993881922095)
XLA Ops:
  11.4 5.2 all-gather
  16.7 4.4 all-gather.1
  27.6 7.1 copy.178
  34.7 6.6 slice.39
  41.3 13.2 %reshape.303 = f32[3,512,1023]{2,1,0:T(8,128)} reshape(f32[3,523776]{1,0:T(4,128)} %slice.39) | data formatting | bytes 12570624 | tf_op jit(solution)/shard_map/reshape | solution.py:42
  70.7 8.0 all-to-all-done
  88.4 4.0 all-to-all-start.1
  117.3 4.5 all_gather.44
  132.9 4.2 gather_fusion.2
  140.9 44.0 %all-gather.13.cloned.1.call-done = bf16[1280,4,768]{2,0,1:T(8,128)(2,1)} async-done(((bf16[80,4,768]{2,0,1:T(8,128)(2,1)}), bf16[1280,4,768]{2,0,1:T(8,128)(2,1)}) %all-gather.13.cloned.1.call-update) | async-done | bytes 7864336 | tf_op jit(solution)/shard_map/all_gather | solution.py:163
  184.9 8.1 fusion.63
  193.1 14.4 %all-gather.17.cloned.1.call-done = bf16[4,192,768]{2,1,0:T(8,128)(2,1)} async-done(((bf16[4,192,384]{2,1,0:T(8,128)(2,1)}), bf16[4,192,768]{2,1,0:T(8,128)(2,1)}) %all-gather.17.cloned.1.call-update) | async-done | bytes 1179664 | tf_op jit(solution)/shard_map/all_gather | solution.py:95
  207.5 10.3 %convolution_bitcast_fusion.1 = f32[1280,4,768]{2,0,1:T(8,128)} fusion(bf16[4,192,768]{2,1,0:T(8,128)(2,1)} %all-gather.17.cloned.1.call-done, f32[4,1280,192]{1,2,0:T(8,128)} %fusion.63), kind=kOutput, calls=%fused_computation.6 | convolution fusion | flops 1518796800 | bytes 20840448 | tf_op jit(solution)/shard_map/sef,efd->sed/dot_general | solution.py:168
  218.0 63.8 %all-gather.19.cloned.1.call-done = bf16[1280,4,768]{2,0,1:T(8,128)(2,1)} async-done(((bf16[80,4,768]{2,0,1:T(8,128)(2,1)}), bf16[1280,4,768]{2,0,1:T(8,128)(2,1)}) %all-gather.19.cloned.1.call-update) | async-done | bytes 7864336 | tf_op jit(solution)/shard_map/all_gather | solution.py:201
  281.9 8.6 fusion.6
  291.7 10.6 %convolution_bitcast_fusion = f32[1280,4,768]{2,0,1:T(8,128)} fusion(bf16[1280,4,192]{0,2,1:T(8,128)(2,1)S(1)} %fusion.6, bf16[4,768,192]{1,2,0:T(8,128)(2,1)S(1)} %copy-done.7), kind=kOutput, calls=%fused_computation.5 | convolution fusion | flops 1509949440 | bytes 18874368 | tf_op jit(solution)/shard_map/sef,edf->sed/dot_general | solution.py:213
  303.6 9.7 %all_gather.50 = bf16[512,768]{1,0:T(8,128)(2,1)} all-gather(bf16[128,768]{1,0:T(8,128)(2,1)} %copy-done.19), channel_id=1, replica_groups=mesh['fsdp'=2,'ctx'=4,'tp'=4] {'ctx'}, dimensions={0}, use_global_device_ids=true | all-gather | bytes 983040 | tf_op jit(solution)/shard_map/all_gather | solution.py:240
  314.0 127.2 %reduce-scatter.10.cloned.1.call-done = f32[80,4,768]{2,0,1:T(8,128)} async-done(((f32[1280,4,768]{2,0,1:T(8,128)}), f32[80,4,768]{2,0,1:T(8,128)}) %reduce-scatter.10.cloned.1.call-update) | async-done | bytes 983056 | tf_op jit(solution)/shard_map/reduce_scatter | solution.py:167
  459.1 142.7 %reduce-scatter.12.cloned.1.call-done = f32[80,4,768]{2,0,1:T(8,128)} async-done(((f32[1280,4,768]{2,0,1:T(8,128)}), f32[80,4,768]{2,0,1:T(8,128)}) %reduce-scatter.12.cloned.1.call-update) | async-done | bytes 983056 | tf_op jit(solution)/shard_map/reduce_scatter | solution.py:212
  620.4 8.6 all_gather.49
  648.1 28.3 %reduce-scatter.14.cloned.1.call-done = f32[384,3,3,64]{0,3,2,1:T(8,128)} async-done(((f32[768,3,3,64]{0,3,2,1:T(8,128)}), f32[384,3,3,64]{0,3,2,1:T(8,128)}) %reduce-scatter.14.cloned.1.call-update) | async-done | bytes 884752 | tf_op jit(solution)/shard_map/reduce_scatter | solution.py:322
  679.5 7.0 fusion.67
  688.0 7.8 fusion.57
  703.3 7.6 reshape.380
  710.9 5.7 reshape.314
  718.7 4.4 all-to-all-start.2
  723.1 4.6 pad_convert_fusion
  734.8 39.7 %psum.45 = f32[12,32]{1,0:T(8,128)} all-reduce(f32[12,32]{1,0:T(8,128)S(1)} %dynamic_update_slice.22), channel_id=1, replica_groups=mesh['fsdp'=2,'ctx'=4,'tp'=4] {'fsdp','ctx','tp'}, use_global_device_ids=true, to_apply=%region_30.31 | all-reduce | flops 384 | bytes 3072 | tf_op jit(solution)/shard_map/psum | solution.py:345
  786.7 5.3 all-reduce.9
  792.1 60.5 %all-reduce.7 = (f32[384]{0:T(512)}, f32[384]{0:T(512)}, f32[384,4]{0,1:T(4,128)}) all-reduce(f32[384]{0:T(512)S(1)} %dynamic-slice.3, f32[384]{0:T(512)S(1)} %dynamic-slice.5, f32[384,4]{0,1:T(4,128)S(1)} %copy.175), channel_id=1, replica_groups=mesh['fsdp'=2,'ctx'=4,'tp'=4] {'ctx','tp'}, use_global_device_ids=true, to_apply=%region_24.25 | all-reduce | flops 2304 | bytes 18432 | tf_op jit(solution)/shard_map/psum | solution.py:344
  855.4 5.2 copy.164
  860.6 28.8 %reduce-scatter.20.cloned.1.call-done = f32[4,192,384]{2,1,0:T(8,128)} async-done(((f32[4,192,768]{2,1,0:T(8,128)}), f32[4,192,384]{2,1,0:T(8,128)}) %reduce-scatter.20.cloned.1.call-update) | async-done | bytes 1179664 | tf_op jit(solution)/shard_map/reduce_scatter | solution.py:327
  (251 shorter events, 171.7 us)
Async XLA Ops:
  7.2 14.6 %copy-start = (f32[12,32]{1,0:T(8,128)S(1)}, f32[12,32]{1,0:T(8,128)}, u32[]{:S(2)}) copy-start(f32[12,32]{1,0:T(8,128)} %param.19) | copy-start | bytes 4612
  7.2 13.9 %copy-start.43 = (s32[31]{0:T(128)S(1)}, s32[31]{0:T(128)}, u32[]{:S(2)}) copy-start(s32[31]{0:T(128)} %constant.127.clone) | copy-start | bytes 376
  7.2 9.4 %copy-start.42 = (bf16[384]{0:T(512)(128)(2,1)S(1)}, bf16[384]{0:T(512)(128)(2,1)}, u32[]{:S(2)}) copy-start(bf16[384]{0:T(512)(128)(2,1)} %param.20) | copy-start | bytes 2308
  7.2 54.5 %all-gather.9.cloned.1.call-start = ((), (), s32[]{:S(2)}) async-start(), calls=%async_computation.10 | async-start | bytes 5308416 | tf_op jit(solution)/shard_map/all_gather | solution.py:90
  8.0 93.8 %all-gather.11.cloned.1.call-start = ((), (), s32[]{:S(2)}) async-start(), calls=%async_computation.11 | async-start | bytes 1769472 | tf_op jit(solution)/shard_map/all_gather | solution.py:91
  8.7 132.2 %all-gather.15.cloned.1.call-start = ((), (), s32[]{:S(2)}) async-start(), calls=%async_computation.13 | async-start | bytes 1769472 | tf_op jit(solution)/shard_map/all_gather | solution.py:94
  11.4 47.4 %copy-start.36 = (f32[128]{0:T(128)}, f32[128]{0:T(128)S(1)}, u32[]{:S(2)}) copy-start(f32[128]{0:T(128)S(1)} %get-tuple-element.139) | copy-start | bytes 1540
  16.7 42.1 %copy-start.26 = (f32[768]{0:T(1024)}, f32[768]{0:T(1024)S(1)}, u32[]{:S(2)}) copy-start(f32[768]{0:T(1024)S(1)} %reshape.367) | copy-start | bytes 9220
  60.8 9.1 %copy-start.33 = (s32[1,512]{1,0:T(1,128)S(1)}, s32[1,512]{1,0:T(1,128)}, u32[]{:S(2)}) copy-start(s32[1,512]{1,0:T(1,128)} %param.14) | copy-start | bytes 6148
  65.6 13.2 %all-to-all-start = ((bf16[128,3,12,64]{0,3,1,2:T(8,128)(2,1)}), bf16[128,3,12,64]{0,3,1,2:T(8,128)(2,1)S(1)}, u32[]{:S(2)}, u32[]{:S(2)}) async-start(bf16[128,3,12,64]{0,3,1,2:T(8,128)(2,1)} %copy.136), calls=%async_computation | async-start | bytes 1179648 | tf_op jit(solution)/shard_map/all_to_all | solution.py:104
  85.3 18.9 %copy-start.22 = (bf16[3,64,512]{2,1,0:T(8,128)(2,1)}, bf16[3,64,512]{2,1,0:T(8,128)(2,1)S(1)}, u32[]{:S(2)}) copy-start(bf16[3,64,512]{2,1,0:T(8,128)(2,1)S(1)} %fusion.19) | copy-start | bytes 589828
  88.4 9.4 %all-to-all-start.1 = ((bf16[4,2,12288]{2,1,0:T(2,128)(2,1)}), bf16[4,2,12288]{2,1,0:T(2,128)(2,1)}, u32[]{:S(2)}, u32[]{:S(2)}) async-start(bf16[4,2,12288]{2,1,0:T(2,128)(2,1)} %reshape.382), calls=%async_computation.1 | async-start | bytes 393216 | tf_op jit(solution)/shard_map/all_to_all | solution.py:146
  92.4 92.5 %all-gather.13.cloned.1.call-start = ((), (), s32[]{:S(2)}) async-start(), calls=%async_computation.12 | async-start | bytes 8355840 | tf_op jit(solution)/shard_map/all_gather | solution.py:163
  93.2 15.0 %copy-start.24 = (f32[768]{0:T(1024)}, f32[768]{0:T(1024)S(1)}, u32[]{:S(2)}) copy-start(f32[768]{0:T(1024)S(1)} %reshape.368) | copy-start | bytes 9220
  112.0 95.5 %all-gather.17.cloned.1.call-start = ((), (), s32[]{:S(2)}) async-start(), calls=%async_computation.14 | async-start | bytes 1769472 | tf_op jit(solution)/shard_map/all_gather | solution.py:95
  112.6 169.3 %all-gather.19.cloned.1.call-start = ((), (), s32[]{:S(2)}) async-start(), calls=%async_computation.16 | async-start | bytes 8355840 | tf_op jit(solution)/shard_map/all_gather | solution.py:201
  121.7 15.3 %copy-start.28 = (bf16[768,4]{0,1:T(4,128)(2,1)}, bf16[768,4]{0,1:T(4,128)(2,1)S(1)}, u32[]{:S(2)}) copy-start(bf16[768,4]{0,1:T(4,128)(2,1)S(1)} %all_gather.44) | copy-start | bytes 18436
  140.9 300.3 %reduce-scatter.10.cloned.1.call-start = ((), (), s32[]{:S(2)}) async-start(), calls=%async_computation.15 | async-start | bytes 16711680 | tf_op jit(solution)/shard_map/reduce_scatter | solution.py:167
  217.8 384.0 %reduce-scatter.12.cloned.1.call-start = ((), (), s32[]{:S(2)}) async-start(), calls=%async_computation.17 | async-start | bytes 16711680 | tf_op jit(solution)/shard_map/reduce_scatter | solution.py:212
  281.9 9.8 %copy-start.7 = (bf16[4,768,192]{1,2,0:T(8,128)(2,1)S(1)}, bf16[4,768,192]{1,2,0:T(8,128)(2,1)}, u32[]{:S(2)}) copy-start(bf16[4,768,192]{1,2,0:T(8,128)(2,1)} %all-gather.15.cloned.1.call-done) | copy-start | bytes 3538948
  302.3 343.0 %reduce-scatter.16.cloned.1.call-start = ((), (), s32[]{:S(2)}) async-start(), calls=%async_computation.19 | async-start | bytes 884736 | tf_op jit(solution)/shard_map/reduce_scatter | solution.py:323
  616.0 13.8 %copy-start.23 = (bf16[3,64,512]{2,1,0:T(8,128)(2,1)S(1)}, bf16[3,64,512]{2,1,0:T(8,128)(2,1)}, u32[]{:S(2)}) copy-start(bf16[3,64,512]{2,1,0:T(8,128)(2,1)} %copy-done.22) | copy-start | bytes 589828
  631.0 45.4 %reduce-scatter.14.cloned.1.call-start = ((), (), s32[]{:S(2)}) async-start(), calls=%async_computation.18 | async-start | bytes 2654208 | tf_op jit(solution)/shard_map/reduce_scatter | solution.py:322
  640.2 134.3 %reduce-scatter.22.cloned.1.call-start = ((), (), s32[]{:S(2)}) async-start(), calls=%async_computation.22 | async-start | bytes 589824
  641.4 214.0 %all-reduce.12.cloned.1.call-start = ((), (), s32[]{:S(2)}) async-start(), calls=%async_computation.23 | async-start | bytes 9437184 | tf_op jit(solution)/shard_map/psum | solution.py:344
  679.5 181.2 %reduce-scatter.18.cloned.1.call-start = ((), (), s32[]{:S(2)}) async-start(), calls=%async_computation.20 | async-start | bytes 3538944 | tf_op jit(solution)/shard_map/reduce_scatter | solution.py:326
  686.5 202.9 %reduce-scatter.20.cloned.1.call-start = ((), (), s32[]{:S(2)}) async-start(), calls=%async_computation.21 | async-start | bytes 3538944 | tf_op jit(solution)/shard_map/reduce_scatter | solution.py:327
  718.7 56.8 %all-to-all-start.2 = ((bf16[4,2,36864]{2,1,0:T(2,128)(2,1)}), bf16[4,2,36864]{2,1,0:T(2,128)(2,1)}, u32[]{:S(2)}, u32[]{:S(2)}) async-start(bf16[4,2,36864]{2,1,0:T(2,128)(2,1)} %reshape.384), calls=%async_computation.4 | async-start | bytes 1179648 | tf_op jit(solution)/shard_map/all_to_all | solution.py:298
  731.0 51.8 %copy-start.4 = (bf16[768,2304]{1,0:T(8,128)(2,1)S(1)}, bf16[768,2304]{1,0:T(8,128)(2,1)}, u32[]{:S(2)}) copy-start(bf16[768,2304]{1,0:T(8,128)(2,1)} %all-gather.9.cloned.1.call-done) | copy-start | bytes 10616836
  731.0 51.8 %copy-start.27 = (f32[768]{0:T(1024)S(1)}, f32[768]{0:T(1024)}, u32[]{:S(2)}) copy-start(f32[768]{0:T(1024)} %copy-done.26) | copy-start | bytes 9220
  855.4 35.1 %copy-start.1 = (f32[12,32]{1,0:T(8,128)S(1)}, f32[12,32]{1,0:T(8,128)}, u32[]{:S(2)}) copy-start(f32[12,32]{1,0:T(8,128)} %param.19) | copy-start | bytes 4612
  855.4 34.1 %copy-start.20 = (f32[768,384]{1,0:T(8,128)S(1)}, f32[768,384]{1,0:T(8,128)}, u32[]{:S(2)}) copy-start(f32[768,384]{1,0:T(8,128)} %get-tuple-element.156) | copy-start | bytes 3538948
  (31 other events, 93.1 us)
Sparse Core Ops, SparseCore 0:
  9.6 52.0 all-gather.8
  63.3 22.7 all-gather.10
  87.7 22.7 all-gather.14
  113.3 71.5 all-gather.12
  186.3 21.1 all-gather.16
  210.2 71.5 all-gather.18
  286.0 155.1 reduce-scatter.9
  445.8 155.9 reduce-scatter.11
  631.1 14.1 reduce-scatter.15
  648.1 28.2 reduce-scatter.13
  678.6 13.0 reduce-scatter.21
  696.3 118.0 all-reduce.11
  817.3 34.6 reduce-scatter.17
  854.7 34.7 reduce-scatter.19
where the time goes:
time: 905 us; the launch traced here: 897 us
  waiting for transfers between devices  468 us (52%)
  local copies, waits for them, and re-layouts  146 us (16%)
  blocking collectives  138 us (15%)
  matrix products  79.4 us (9%)
  other arithmetic  37 us (4%)
  between operations  15.4 us (2%)
  starting transfers between devices  13.4 us (1%)
    reduce_scatter x1, waiting for transfers between devices, local(): lax.psum_scatter(jnp.einsum('sef,edf->sed', row_block, up_again, preferre...  143 us
    reduce_scatter x1, waiting for transfers between devices, local(): lax.psum_scatter(jnp.einsum('sef,efd->sed', row_block, down_full, preferr...  127 us
    all_gather x1, waiting for transfers between devices, local(): grad_arrived = lax.all_gather(grad_slots, ('ctx', 'tp'), axis=0, tiled=True)  63.8 us
    psum x1, blocking collectives, local(): lax.psum((shares[0], qkv_placed, proj_placed, shares[3], shares[4]), ('ct...  60.5 us
    unnamed x108, local copies, waits for them, and re-layouts  51.7 us
    all_gather x1, waiting for transfers between devices, local(): arrived = lax.all_gather(dispatched, ('ctx', 'tp'), axis=0, tiled=True)  44 us
    psum x1, blocking collectives, local(): table_grad = lax.psum(table_term, ('fsdp', 'ctx', 'tp'))  39.7 us
    reduce_scatter x1, waiting for transfers between devices, local(): lax.psum_scatter(grad_down, 'fsdp', scatter_dimension=2, tiled=True)  28.8 us
  transfers between devices with their start and end apart: 17, of which 11 were waited for; matrix products, arithmetic and copies ran while one was open for 25% of the time, Pallas kernels for 0%

commit v1 on v0

v1 whole, which is shorter than its diff:
```python
import jax
import jax.numpy as jnp
import numpy as np
from jax import lax
from jax.sharding import PartitionSpec as P

BUCKETS = 32
MAX_DISTANCE = 128
EPSILON = 1e-06
MASK_FILL = -1e30
F32 = jnp.float32
BF16 = jnp.bfloat16


def bucket_bounds(buckets, far_reach):
    exact_count = buckets // 2
    bounds = []
    for number in range(1, buckets):
        if number <= exact_count:
            bounds.append(number)
        else:
            exponent = (number - exact_count) / (buckets - exact_count)
            bounds.append(int(np.ceil(exact_count * (far_reach / exact_count) ** exponent)))
    return bounds


BOUNDS = bucket_bounds(BUCKETS, MAX_DISTANCE)


def rms_scale(values):
    return lax.rsqrt(jnp.mean(values * values, axis=-1, keepdims=True) + EPSILON)


def dot(a, b, ca, cb):
    return lax.dot_general(a, b, (((ca,), (cb,)), ((), ())), preferred_element_type=F32)


def exchange_sum(part, axis, dim):
    count = lax.axis_size(axis)
    size = part.shape[dim] // count
    me = lax.axis_index(axis)
    total = lax.dynamic_slice_in_dim(part, me * size, size, dim)
    for step in range(1, count):
        target = lax.rem(me + step, count)
        piece = lax.dynamic_slice_in_dim(part, target * size, size, dim).astype(BF16)
        total = total + lax.ppermute(
            piece, axis, [(i, (i + step) % count) for i in range(count)]
        ).astype(F32)
    return total


def local(
    tokens,
    seg_ids,
    routes,
    norm_attn,
    weight_qkv,
    weight_proj,
    rel_table,
    norm_ffn,
    weight_router,
    expert_up,
    expert_down,
    cotangent,
):
    rows = tokens.shape[1]
    width = tokens.shape[2]
    heads = rel_table.shape[0]
    head_size = width // heads
    ctx_count = lax.axis_size("ctx")
    heads_here = heads // ctx_count
    hw = heads_here * head_size
    experts = expert_up.shape[0]
    units = expert_up.shape[2]
    length = seg_ids.shape[1]
    score_scale = head_size ** (-0.5)
    ctx_index = lax.axis_index("ctx")
    fsdp_index = lax.axis_index("fsdp")
    own_width = norm_attn.shape[0]
    world = ("ctx", "tp")

    token_group = lax.all_gather(tokens[0], "ctx", axis=0, tiled=True)
    small = jnp.concatenate([norm_attn[None], norm_ffn[None], weight_router.T], axis=0)
    small = lax.all_gather(small, "fsdp", axis=1, tiled=True)
    gain_one = small[0].astype(F32)
    gain_two = small[1].astype(F32)
    router_t = small[2:]
    qkv_part = jnp.concatenate(
        [
            lax.dynamic_slice_in_dim(weight_qkv, s * width + ctx_index * hw, hw, 1)
            for s in range(3)
        ],
        axis=1,
    )
    qkv_here = lax.all_gather(qkv_part, "fsdp", axis=0, tiled=True)
    proj_full = lax.all_gather(weight_proj, "fsdp", axis=1, tiled=True)
    route_all = lax.all_gather(routes[0], world, axis=0, tiled=True)
    up_t = lax.all_gather(
        jnp.swapaxes(expert_up, 1, 2).reshape(experts * units, own_width),
        "fsdp",
        axis=1,
        tiled=True,
    )
    down = lax.all_gather(
        expert_down.reshape(experts * units, own_width), "fsdp", axis=1, tiled=True
    )
    grad_all = lax.all_gather(cotangent[0], world, axis=0, tiled=True)

    block = MAX_DISTANCE
    table_here = lax.dynamic_slice_in_dim(rel_table, ctx_index * heads_here, heads_here, 0)
    offset = (
        lax.broadcasted_iota(jnp.int32, (1, block, block), 1)
        - lax.broadcasted_iota(jnp.int32, (1, block, block), 2)
    )

    def bias_block(distance):
        value = jnp.broadcast_to(table_here[:, 0][:, None, None], (heads_here, block, block))
        for number, bound in enumerate(BOUNDS, 1):
            value = jnp.where(distance >= bound, table_here[:, number][:, None, None], value)
        return value

    near = bias_block(offset)
    next_near = bias_block(offset + block)
    far = jnp.broadcast_to(table_here[:, BUCKETS - 1][:, None, None], (heads_here, block, block))
    blocks = length // block
    picks = {0: near, 1: next_near}
    bias = jnp.concatenate(
        [
            jnp.concatenate(
                [picks.get(i - j, far) for j in range(blocks)],
                axis=2,
            )
            for i in range(blocks)
        ],
        axis=1,
    )
    positions = jnp.arange(length, dtype=jnp.int32)
    segment = seg_ids[0]
    allowed = (segment[:, None] == segment[None, :]) & (positions[:, None] >= positions[None, :])
    bias = jnp.where(allowed[None], bias, MASK_FILL)

    inputs_group = token_group.astype(F32)
    normed_group = (inputs_group * rms_scale(inputs_group) * gain_one).astype(BF16)
    projected = dot(normed_group, qkv_here, 1, 0).astype(BF16)
    by_head = projected.reshape(length, 3, heads_here, head_size)
    query, key, value = by_head[:, 0], by_head[:, 1], by_head[:, 2]

    scores = (
        jnp.einsum("qhd,khd->hqk", query, key, preferred_element_type=F32) * score_scale + bias
    )
    peak = jnp.max(scores, axis=-1, keepdims=True)
    weights = jnp.exp(scores - peak)
    probs = weights / jnp.sum(weights, axis=-1, keepdims=True)
    low_probs = probs.astype(BF16)
    attended = (
        jnp.einsum("hqk,khd->qhd", low_probs, value, preferred_element_type=F32)
        .astype(BF16)
        .reshape(length, hw)
    )
    mixed = lax.all_to_all(attended, "ctx", split_axis=0, concat_axis=1, tiled=True)
    inputs = tokens[0].astype(F32)
    scale_one = rms_scale(inputs)
    middle = inputs + dot(mixed, proj_full, 1, 0)
    scale_two = rms_scale(middle)
    normed_two = (middle * scale_two * gain_two).astype(BF16)

    normed_all = lax.all_gather(normed_two, world, axis=0, tiled=True)

    def gates_of(normed, route):
        logits = dot(normed, router_t, 1, 1)
        number = lax.broadcasted_iota(jnp.int32, (1, experts), 1)
        chosen = (route[:, 0:1] == number) | (route[:, 1:2] == number)
        masked = jnp.where(chosen, logits, MASK_FILL)
        raw = jnp.where(chosen, jnp.exp(masked - jnp.max(masked, axis=1, keepdims=True)), 0.0)
        return raw / jnp.sum(raw, axis=1, keepdims=True)

    gates_all = gates_of(normed_all, route_all)
    column = lax.broadcasted_iota(jnp.int32, (1, experts * units), 1) // units
    spread = gates_all[:, 0:1]
    for e in range(1, experts):
        spread = jnp.where(column >= e, gates_all[:, e : e + 1], spread)
    pre = dot(normed_all, up_t, 1, 1)
    reach = dot(grad_all, down, 1, 1)
    act, gelu_back = jax.vjp(jax.nn.gelu, pre)
    act = act.astype(BF16).astype(F32)
    gated = (act * spread).astype(BF16)
    product = act * reach
    dots_all = jnp.stack(
        [
            jnp.sum(jnp.where(column == e, product, 0.0), axis=1)
            for e in range(experts)
        ],
        axis=0,
    )
    grad_pre = gelu_back(reach * spread)[0].astype(BF16)
    total_rows = normed_all.shape[0]
    devices = total_rows // rows
    dots_all = jnp.swapaxes(dots_all.reshape(experts, devices, rows), 0, 1)
    dots_own = lax.psum_scatter(
        dots_all.reshape(devices, experts * rows), world, scatter_dimension=0, tiled=True
    )
    gate_dots = dots_own.reshape(experts, rows).T
    grad_normed_two = lax.psum_scatter(
        dot(grad_pre, up_t, 1, 0).astype(BF16), world, scatter_dimension=0, tiled=True
    ).astype(F32)
    result = lax.psum_scatter(
        dot(gated, down, 1, 0).astype(BF16), world, scatter_dimension=0, tiled=True
    ).astype(F32)
    output = (middle + result).astype(BF16)[None]
    grad_up = exchange_sum(dot(grad_pre, normed_all, 0, 0), "fsdp", 1)
    grad_up = jnp.swapaxes(grad_up.reshape(experts, units, own_width), 1, 2)
    grad_down = exchange_sum(dot(gated, grad_all, 0, 0), "fsdp", 1)
    grad_down = grad_down.reshape(experts, units, own_width)

    grad_out = cotangent[0].astype(F32)
    gates = gates_of(normed_two, routes[0])
    grad_logits = gates * (gate_dots - jnp.sum(gates * gate_dots, axis=1, keepdims=True))
    grad_normed_two = grad_normed_two + jnp.dot(
        grad_logits, router_t.astype(F32), precision=lax.Precision.HIGHEST
    )
    grad_router = lax.dot_general(
        grad_logits,
        normed_two.astype(F32),
        (((0,), (0,)), ((), ())),
        precision=lax.Precision.HIGHEST,
    )
    weighted_two = grad_normed_two * gain_two
    grad_gain_two = jnp.sum(grad_normed_two * middle * scale_two, axis=0)
    grad_middle = (
        grad_out
        + scale_two * weighted_two
        - middle * scale_two**3 * jnp.mean(weighted_two * middle, axis=1, keepdims=True)
    )
    grad_mid_group = lax.all_gather(grad_middle.astype(BF16), "ctx", axis=0, tiled=True)

    proj_rows = lax.dynamic_slice_in_dim(proj_full, ctx_index * hw, hw, 0)
    grad_attended = dot(grad_mid_group, proj_rows, 1, 1).astype(BF16)
    grad_heads = grad_attended.reshape(length, heads_here, head_size)
    grad_value = jnp.einsum("hqk,qhd->khd", low_probs, grad_heads, preferred_element_type=F32)
    grad_probs = jnp.einsum("qhd,khd->hqk", grad_heads, value, preferred_element_type=F32)
    grad_scores = (
        probs * (grad_probs - jnp.sum(probs * grad_probs, axis=-1, keepdims=True))
    ).astype(BF16)
    grad_query = (
        jnp.einsum("hqk,khd->qhd", grad_scores, key, preferred_element_type=F32) * score_scale
    )
    grad_key = (
        jnp.einsum("hqk,qhd->khd", grad_scores, query, preferred_element_type=F32) * score_scale
    )
    grad_qkv = jnp.concatenate(
        [
            grad_query.astype(BF16).reshape(length, hw),
            grad_key.astype(BF16).reshape(length, hw),
            grad_value.astype(BF16).reshape(length, hw),
        ],
        axis=1,
    )
    grad_normed_one = exchange_sum(dot(grad_qkv, qkv_here, 1, 1), "ctx", 0)

    weight_part = jnp.concatenate(
        [dot(normed_group, grad_qkv, 0, 0), dot(grad_mid_group, attended, 0, 0)], axis=1
    )
    weight_own = lax.psum_scatter(
        weight_part.astype(BF16), ("fsdp", "tp"), scatter_dimension=0, tiled=True
    )
    weight_all = lax.all_gather(weight_own, world, axis=0, tiled=True).astype(F32)
    weight_all = weight_all.reshape(ctx_count, own_width, 4 * hw)
    grad_weight_qkv = jnp.concatenate(
        [
            weight_all[c, :, s * hw : (s + 1) * hw]
            for s in range(3)
            for c in range(ctx_count)
        ],
        axis=1,
    )
    grad_weight_proj = jnp.swapaxes(weight_all[:, :, 3 * hw :], 1, 2).reshape(width, own_width)

    def score_block(i, j):
        return grad_scores[
            :, i * block : (i + 1) * block, j * block : (j + 1) * block
        ].astype(F32)

    near_sum = sum(score_block(i, i) for i in range(blocks))
    next_sum = sum(score_block(i + 1, i) for i in range(blocks - 1))
    far_sum = sum(
        jnp.sum(score_block(i, j), axis=(1, 2)) for i in range(blocks) for j in range(i - 1)
    )
    lows = [0] + BOUNDS
    highs = BOUNDS + [2 * block]
    bucket_sums = [
        jnp.sum(jnp.where((offset >= lo) & (offset < hi), near_sum, 0.0), axis=(1, 2))
        + jnp.sum(
            jnp.where((offset + block >= lo) & (offset + block < hi), next_sum, 0.0), axis=(1, 2)
        )
        for lo, hi in zip(lows, highs)
    ]
    bucket_sums[-1] = bucket_sums[-1] + far_sum
    table_here_grad = jnp.stack(bucket_sums, axis=1)
    table_term = lax.dynamic_update_slice_in_dim(
        jnp.zeros((heads, BUCKETS), F32), table_here_grad, ctx_index * heads_here, 0
    )

    weighted_one = grad_normed_one * gain_one
    grad_gain_one = jnp.sum(grad_normed_one * inputs * scale_one, axis=0)
    grad_tokens = (
        grad_middle
        + scale_one * weighted_one
        - inputs * scale_one**3 * jnp.mean(weighted_one * inputs, axis=1, keepdims=True)
    )
    packed = jnp.concatenate(
        [
            grad_gain_one,
            grad_gain_two,
            grad_router.reshape(-1),
            table_term.reshape(-1),
        ]
    ).reshape(-1, 128)
    packed = lax.psum(packed, ("fsdp", "ctx", "tp")).reshape(-1)
    gains = packed[: (2 + experts) * width].reshape(2 + experts, width)
    gains = lax.dynamic_slice_in_dim(gains, fsdp_index * own_width, own_width, 1)
    table_grad = packed[(2 + experts) * width :].reshape(heads, BUCKETS)
    return (
        output,
        grad_tokens[None],
        gains[0],
        grad_weight_qkv,
        grad_weight_proj,
        table_grad,
        gains[1],
        gains[2:].T,
        grad_up,
        grad_down,
    )


def solution(mesh):
    rows = P(("fsdp", "tp"), "ctx", None)
    in_specs = (
        rows,
        P(("fsdp", "tp"), None),
        rows,
        P("fsdp"),
        P("fsdp", None),
        P(None, "fsdp"),
        P(),
        P("fsdp"),
        P("fsdp", None),
        P(None, "fsdp", ("ctx", "tp")),
        P(None, ("ctx", "tp"), "fsdp"),
        rows,
    )
    out_specs = (
        rows,
        rows,
        P("fsdp"),
        P("fsdp", None),
        P(None, "fsdp"),
        P(),
        P("fsdp"),
        P("fsdp", None),
        P(None, "fsdp", ("ctx", "tp")),
        P(None, ("ctx", "tp"), "fsdp"),
    )
    return jax.shard_map(local, mesh=mesh, in_specs=in_specs, out_specs=out_specs, check_vma=False)
```

time: 905 us -> 542 us (0.60)
  waiting for transfers between devices: 468 us -> 162 us
  local copies, waits for them, and re-layouts: 146 us -> 31 us
  blocking collectives: 138 us -> 183 us
  other arithmetic: 37 us -> 64.2 us
    reduce_scatter x6 -> x3, waiting for transfers between devices: 331 us -> 56.3 us  [the longest x1 42.9 us: local(): lax.psum_scatter(weight_part.astype(BF16), ('fsdp', 'tp'), scatter_dimens...]
    psum x2 -> x1, blocking collectives: 100 us -> 40.1 us  [local(): packed = lax.psum(packed, ('fsdp', 'ctx', 'tp')).reshape(-1)]
    unnamed x1, blocking collectives: 5.3 us -> 60.7 us
    all_gather x5, blocking collectives: 32.4 us -> 73.7 us  [the longest x1 31.7 us: local(): route_all = lax.all_gather(routes[0], world, axis=0, tiled=True)]
    unnamed x108 -> x162, local copies, waits for them, and re-layouts: 51.7 us -> 10.5 us
    reshape x11 -> x4, local copies, waits for them, and re-layouts: 37.3 us -> 2.07 us  [the longest x1 1.31 us: local(): grad_router.reshape(-1)]
    all_gather x6, waiting for transfers between devices: 123 us -> 94.4 us  [the longest x1 47.4 us: local(): grad_all = lax.all_gather(cotangent[0], world, axis=0, tiled=True)]
    and x0 -> x32, other arithmetic: none -> 20 us  [the longest x16 10.1 us: local(): (offset >= lo) & (offset < hi)]
  transfers between devices with their start and end apart: 17 -> 14, of which waited for: 11 -> 9; matrix products, arithmetic and copies ran while one was open for 25% -> 21% of each run, Pallas kernels for 0% -> 0%
where the time goes in v1:
time: 542 us; the launch traced here: 535 us
  blocking collectives  183 us (34%)
  waiting for transfers between devices  162 us (30%)
  matrix products  73.5 us (14%)
  other arithmetic  64.2 us (12%)
  local copies, waits for them, and re-layouts  31 us (6%)
  between operations  15.7 us (3%)
  starting transfers between devices  5.87 us (1%)
    unnamed x1, blocking collectives  60.7 us
    dot_general x14, matrix products, dot(): lax.dot_general(a, b, (((ca,), (cb,)), ((), ())), preferred_element_type=...  55.1 us
    all_gather x1, waiting for transfers between devices, local(): grad_all = lax.all_gather(cotangent[0], world, axis=0, tiled=True)  47.4 us
    reduce_scatter x1, waiting for transfers between devices, local(): lax.psum_scatter(weight_part.astype(BF16), ('fsdp', 'tp'), scatter_dimens...  42.9 us
    psum x1, blocking collectives, local(): packed = lax.psum(packed, ('fsdp', 'ctx', 'tp')).reshape(-1)  40.1 us
    all_gather x1, blocking collectives, local(): route_all = lax.all_gather(routes[0], world, axis=0, tiled=True)  31.7 us
    all_gather x1, blocking collectives, local(): qkv_here = lax.all_gather(qkv_part, 'fsdp', axis=0, tiled=True)  20.5 us
    all_gather x1, waiting for transfers between devices, local(): lax.all_gather(jnp.swapaxes(expert_up, 1, 2).reshape(experts * units, own...  19.6 us
  transfers between devices with their start and end apart: 14, of which 9 were waited for; matrix products, arithmetic and copies ran while one was open for 21% of the time, Pallas kernels for 0%

profile of v1, /device:TPU:0, one launch (start us, length us, event | category | flops | bytes accessed | tf_op | source)
XLA Modules:
  0.0 534.9 jit_solution(10073200459211450725)
XLA Ops:
  11.4 20.5 %all_gather.35 = bf16[768,576]{1,0:T(8,128)(2,1)S(1)} all-gather(bf16[384,576]{1,0:T(8,128)(2,1)S(1)} %pad_maximum_fusion.2), channel_id=1, replica_groups=mesh['fsdp'=2,'ctx'=4,'tp'=4] {'fsdp'}, dimensions={0}, use_global_device_ids=true | all-gather | bytes 1327104 | tf_op jit(solution)/shard_map/all_gather | solution.py:95
  32.0 4.9 all_gather.34
  37.6 8.4 %all-gather = bf16[1,512,768]{2,1,0:T(8,128)(2,1)S(1)} all-gather(bf16[1,128,768]{2,1,0:T(8,128)(2,1)S(1)} %copy-done.6), channel_id=2, replica_groups=mesh['fsdp'=2,'ctx'=4,'tp'=4] {'ctx'}, dimensions={1}, use_global_device_ids=true | all-gather | bytes 983040 | tf_op jit(solution)/shard_map/all_gather | solution.py:82
  51.6 4.9 convolution_convert_fusion.6
  56.7 8.4 %all_to_all.19 = bf16[4,128,192]{1,2,0:T(8,128)(2,1)} all-to-all(bf16[4,128,192]{1,2,0:T(8,128)(2,1)S(1)} %copy.59), channel_id=1, replica_groups=mesh['fsdp'=2,'ctx'=4,'tp'=4] {'ctx'}, dimensions={0} | all-to-all | bytes 393216 | tf_op jit(solution)/shard_map/all_to_all | solution.py:160
  70.2 31.7 %all-gather.1 = s32[1,2048,2]{1,2,0:T(2,128)S(1)} all-gather(s32[1,128,2]{1,2,0:T(2,128)S(1)} %copy-done.68), channel_id=3, replica_groups=mesh['fsdp'=2,'ctx'=4,'tp'=4] {'ctx','tp'}, dimensions={1}, use_global_device_ids=true | all-gather | bytes 17408 | tf_op jit(solution)/shard_map/all_gather | solution.py:97
  104.3 10.7 %all-gather.12.cloned.1.call-done = bf16[2048,768]{1,0:T(8,128)(2,1)} async-done(((bf16[128,768]{1,0:T(8,128)(2,1)}), bf16[2048,768]{1,0:T(8,128)(2,1)}) %all-gather.12.cloned.1.call-update) | async-done | bytes 3145744 | tf_op jit(solution)/shard_map/all_gather | solution.py:167
  115.0 2.8 fusion.257
  118.6 19.6 %all-gather.14.cloned.1.call-done = bf16[768,768]{1,0:T(8,128)(2,1)} async-done(((bf16[768,384]{1,0:T(8,128)(2,1)}), bf16[768,768]{1,0:T(8,128)(2,1)}) %all-gather.14.cloned.1.call-update) | async-done | bytes 1179664 | tf_op jit(solution)/shard_map/all_gather | solution.py:98
  138.2 7.5 %fusion.259 = f32[2048,768]{0,1:T(8,128)} fusion(bf16[2048,768]{1,0:T(8,128)(2,1)} %all-gather.12.cloned.1.call-done, bf16[768,768]{1,0:T(8,128)(2,1)} %all-gather.14.cloned.1.call-done), kind=kOutput, calls=%fused_computation.499 | convolution fusion | flops 2415919104 | bytes 10616832 | tf_op jit(solution)/shard_map/dot_general | solution.py:35
  145.7 16.7 %all-gather.16.cloned.1.call-done = bf16[768,768]{1,0:T(8,128)(2,1)} async-done(((bf16[768,384]{1,0:T(8,128)(2,1)}), bf16[768,768]{1,0:T(8,128)(2,1)}) %all-gather.16.cloned.1.call-update) | async-done | bytes 1179664 | tf_op jit(solution)/shard_map/all_gather | solution.py:104
  162.4 47.4 %all-gather.20.cloned.1.call-done = bf16[1,2048,768]{2,1,0:T(8,128)(2,1)} async-done(((bf16[1,128,768]{2,1,0:T(8,128)(2,1)}), bf16[1,2048,768]{2,1,0:T(8,128)(2,1)}) %all-gather.20.cloned.1.call-update) | async-done | bytes 3145744 | tf_op jit(solution)/shard_map/all_gather | solution.py:107
  209.8 15.3 %select_reduce_fusion.3 = (f32[2048]{0:T(1024)}, f32[2048]{0:T(1024)}, f32[2048]{0:T(1024)}, f32[2048]{0:T(1024)}, bf16[2048,768]{0,1:T(8,128)(2,1)}, /*index=5*/bf16[2048,768]{0,1:T(8,128)(2,1)S(1)}) fusion(pred[768]{0:T(1024)(128)(4,1)} %get-tuple-element.174, pred[768]{0:T(1024)(128)(4,1)} %get-tuple-element.175, pred[768]{0:T(1024)(128)(4,1)} %get-tuple-element.170, ...), kind=kOutput, calls=%fused_computation.16 | convolution fusion | flops 2472534016 | bytes 16979200 | tf_op jit(solution)/shard_map/dot_general | solution.py:35
  226.8 4.1 convolution_convert_fusion
  249.7 7.5 %convolution_convert_fusion.1 = bf16[2048,768]{1,0:T(8,128)(2,1)} fusion(bf16[768,768]{1,0:T(8,128)(2,1)} %all-gather.16.cloned.1.call-done, bf16[2048,768]{0,1:T(8,128)(2,1)} %get-tuple-element.126, f32[2048]{0:T(1024)S(1)} %bitcast.258, f32[2048]{0:T(1024)} %bitcast.261, f32[2048]{0:T(1024)} %bitcast.264, f32[2048]{0:T(1024)S(1)} %bitcast.255, ...), kind=kOutput, calls=%fused_computation.20 | convolution fusion | flops 2426929152 | bytes 7506176 | tf_op jit(solution)/shard_map/dot_general | solution.py:35
  263.4 6.3 %fusion.10 = f32[768,768]{1,0:T(8,128)S(1)} fusion(bf16[1,2048,768]{2,1,0:T(8,128)(2,1)} %all-gather.20.cloned.1.call-done, bf16[2048,768]{0,1:T(8,128)(2,1)} %get-tuple-element.126, f32[2048]{0:T(1024)} %bitcast.259, f32[2048]{0:T(1024)} %bitcast.262, f32[2048]{0:T(1024)} %bitcast.265, f32[2048]{0:T(1024)} %bitcast.256, ...), kind=kOutput, calls=%fused_computation.23 | convolution fusion | flops 2425356288 | bytes 8685824 | tf_op jit(solution)/shard_map/dot_general | solution.py:35
  272.2 2.6 fusion.260
  277.8 60.7 %all-reduce = f32[16,512]{1,0:T(8,128)} all-reduce(f32[16,512]{1,0:T(8,128)} %bitcast.247), channel_id=7, replica_groups=mesh['fsdp'=2,'ctx'=4,'tp'=4] {'ctx','tp'}, use_global_device_ids=true, to_apply=%region_14.15.clone | all-reduce | flops 8192 | bytes 65536
  344.1 2.7 convert_add_fusion
  346.8 2.2 convert_add_fusion.1
  349.0 2.8 multiply_reduce_fusion.1
  351.8 13.4 %reduce-scatter.6.cloned.1.call-done = bf16[128,768]{1,0:T(8,128)(2,1)} async-done(((bf16[2048,768]{1,0:T(8,128)(2,1)}), bf16[128,768]{1,0:T(8,128)(2,1)}) %reduce-scatter.6.cloned.1.call-update) | async-done | bytes 196624 | tf_op jit(solution)/shard_map/reduce_scatter | solution.py:206
  365.2 2.3 fusion.252
  367.4 8.1 %all_gather.42 = bf16[512,768]{1,0:T(8,128)(2,1)S(1)} all-gather(bf16[128,768]{1,0:T(8,128)(2,1)S(1)} %get-tuple-element.124), channel_id=1, replica_groups=mesh['fsdp'=2,'ctx'=4,'tp'=4] {'ctx'}, dimensions={0}, use_global_device_ids=true | all-gather | bytes 983040 | tf_op jit(solution)/shard_map/all_gather | solution.py:234
  379.2 2.7 multiply_convert_fusion.1
  384.3 4.5 convolution_convert_fusion.5
  395.7 2.1 select_reduce_fusion.5
  413.6 42.9 %reduce-scatter.10.cloned.1.call-done = bf16[96,768]{1,0:T(8,128)(2,1)} async-done(((bf16[768,768]{1,0:T(8,128)(2,1)}), bf16[96,768]{1,0:T(8,128)(2,1)}) %reduce-scatter.10.cloned.1.call-update) | async-done | bytes 147472 | tf_op jit(solution)/shard_map/reduce_scatter | solution.py:263
  464.4 3.2 collective-permute-done
  469.1 3.8 collective-permute-done.2
  474.2 40.1 %psum.7 = f32[39,128]{1,0:T(8,128)S(1)} all-reduce(f32[39,128]{1,0:T(8,128)S(1)} %maximum_bitcast_fusion), channel_id=1, replica_groups=mesh['fsdp'=2,'ctx'=4,'tp'=4] {'fsdp','ctx','tp'}, use_global_device_ids=true, to_apply=%region_89.90 | all-reduce | flops 4992 | bytes 39936 | tf_op jit(solution)/shard_map/psum | solution.py:318
  523.2 4.7 concatenate.45
  (392 shorter events, 103.6 us)
Async XLA Ops:
  7.2 24.8 %copy-start.73 = (bf16[384]{0:T(512)(128)(2,1)S(1)}, bf16[384]{0:T(512)(128)(2,1)}, u32[]{:S(2)}) copy-start(bf16[384]{0:T(512)(128)(2,1)} %param.15) | copy-start | bytes 2308
  7.2 24.8 %copy-start.74 = (bf16[384]{0:T(512)(128)(2,1)S(1)}, bf16[384]{0:T(512)(128)(2,1)}, u32[]{:S(2)}) copy-start(bf16[384]{0:T(512)(128)(2,1)} %param.19) | copy-start | bytes 2308
  7.2 24.8 %copy-start.70 = (bf16[384,4]{0,1:T(4,128)(2,1)S(1)}, bf16[384,4]{0,1:T(4,128)(2,1)}, u32[]{:S(2)}) copy-start(bf16[384,4]{0,1:T(4,128)(2,1)} %param.20) | copy-start | bytes 9220
  7.2 30.3 %copy-start.6 = (bf16[1,128,768]{2,1,0:T(8,128)(2,1)S(1)}, bf16[1,128,768]{2,1,0:T(8,128)(2,1)}, u32[]{:S(2)}) copy-start(bf16[1,128,768]{2,1,0:T(8,128)(2,1)} %param.12) | copy-start | bytes 589828
  7.2 57.8 %all-gather.10.cloned.1.call-start = ((), (), s32[]{:S(2)}) async-start(), calls=%async_computation.4 | async-start | bytes 1769472 | tf_op jit(solution)/shard_map/all_gather | solution.py:96
  8.0 107.0 %all-gather.12.cloned.1.call-start = ((), (), s32[]{:S(2)}) async-start(), calls=%async_computation.5 | async-start | bytes 3342336 | tf_op jit(solution)/shard_map/all_gather | solution.py:167
  9.2 37.1 %copy-start.59 = (s32[1,512]{1,0:T(1,128)S(1)}, s32[1,512]{1,0:T(1,128)}, u32[]{:S(2)}) copy-start(s32[1,512]{1,0:T(1,128)} %param.13) | copy-start | bytes 6148
  37.6 29.9 %copy-start.25 = (f32[768]{0:T(1024)}, f32[768]{0:T(1024)S(1)}, u32[]{:S(2)}) copy-start(f32[768]{0:T(1024)S(1)} %get-tuple-element.87) | copy-start | bytes 9220
  51.6 326.2 %copy-start.2 = (f32[3,512,512]{1,2,0:T(8,128)}, f32[3,512,512]{1,2,0:T(8,128)S(1)}, u32[]{:S(2)}) copy-start(f32[3,512,512]{1,2,0:T(8,128)S(1)} %get-tuple-element.160) | copy-start | bytes 9437188
  67.4 36.9 %copy-start.67 = (f32[128]{0:T(128)}, f32[128]{0:T(128)S(1)}, u32[]{:S(2)}) copy-start(f32[128]{0:T(128)S(1)} %get-tuple-element.158) | copy-start | bytes 1540
  68.2 69.9 %all-gather.14.cloned.1.call-start = ((), (), s32[]{:S(2)}) async-start(), calls=%async_computation.6 | async-start | bytes 1769472 | tf_op jit(solution)/shard_map/all_gather | solution.py:98
  69.0 93.4 %all-gather.16.cloned.1.call-start = ((), (), s32[]{:S(2)}) async-start(), calls=%async_computation.7 | async-start | bytes 1769472 | tf_op jit(solution)/shard_map/all_gather | solution.py:104
  69.6 140.2 %all-gather.20.cloned.1.call-start = ((), (), s32[]{:S(2)}) async-start(), calls=%async_computation.11 | async-start | bytes 3342336 | tf_op jit(solution)/shard_map/all_gather | solution.py:107
  70.1 278.8 %reduce-scatter.8.cloned.1.call-start = ((), (), s32[]{:S(2)}) async-start(), calls=%async_computation.9 | async-start | bytes 3342336 | tf_op jit(solution)/shard_map/reduce_scatter | solution.py:203
  118.6 131.1 %copy-start.60 = (f32[2048,1]{0,1:T(1,128)}, f32[2048,1]{0,1:T(1,128)S(1)}, u32[]{:S(2)}) copy-start(f32[2048,1]{0,1:T(1,128)S(1)} %get-tuple-element.147) | copy-start | bytes 24580
  118.6 131.1 %copy-start.61 = (f32[2048,1]{0,1:T(1,128)}, f32[2048,1]{0,1:T(1,128)S(1)}, u32[]{:S(2)}) copy-start(f32[2048,1]{0,1:T(1,128)S(1)} %get-tuple-element.148) | copy-start | bytes 24580
  230.9 134.3 %reduce-scatter.6.cloned.1.call-start = ((), (), s32[]{:S(2)}) async-start(), calls=%async_computation.8 | async-start | bytes 3342336 | tf_op jit(solution)/shard_map/reduce_scatter | solution.py:206
  257.2 199.3 %reduce-scatter.10.cloned.1.call-start = ((), (), s32[]{:S(2)}) async-start(), calls=%async_computation.12 | async-start | bytes 1327104 | tf_op jit(solution)/shard_map/reduce_scatter | solution.py:263
  270.7 73.3 %collective-permute-start.4 = (bf16[768,384]{1,0:T(8,128)(2,1)}, bf16[768,384]{1,0:T(8,128)(2,1)}, u32[]{:S(2)}, u32[]{:S(2)}) collective-permute-start(bf16[768,384]{1,0:T(8,128)(2,1)} %dynamic-slice_convert_fusion), channel_id=1, source_target_pairs={{0,16},{16,0},{1,17},{17,1},{2,18},{18,2},{3,19},{19,3},{4,20},{20... | collective-permute-start | bytes 1769480 | tf_op jit(solution)/shard_map/ppermute | solution.py:46
  276.5 70.3 %collective-permute-start.3 = (bf16[768,384]{1,0:T(8,128)(2,1)}, bf16[768,384]{1,0:T(8,128)(2,1)}, u32[]{:S(2)}, u32[]{:S(2)}) collective-permute-start(bf16[768,384]{1,0:T(8,128)(2,1)} %dynamic-slice_convert_fusion.1), channel_id=1, source_target_pairs={{0,16},{16,0},{1,17},{17,1},{2,18},{18,2},{3,19},{19,3},{4,20},{20... | collective-permute-start | bytes 1769480 | tf_op jit(solution)/shard_map/ppermute | solution.py:46
  277.1 71.9 %copy-start.26 = (f32[768]{0:T(1024)S(1)}, f32[768]{0:T(1024)}, u32[]{:S(2)}) copy-start(f32[768]{0:T(1024)} %copy-done.25) | copy-start | bytes 9220
  391.5 66.4 %copy-start.23 = (bf16[3,64,512]{2,1,0:T(8,128)(2,1)S(1)}, bf16[3,64,512]{2,1,0:T(8,128)(2,1)}, u32[]{:S(2)}) copy-start(bf16[3,64,512]{2,1,0:T(8,128)(2,1)} %fusion.17) | copy-start | bytes 589828
  391.5 66.4 %copy-start.24 = (bf16[3,64,512]{2,1,0:T(8,128)(2,1)S(1)}, bf16[3,64,512]{2,1,0:T(8,128)(2,1)}, u32[]{:S(2)}) copy-start(bf16[3,64,512]{2,1,0:T(8,128)(2,1)} %fusion.18) | copy-start | bytes 589828
  393.0 64.9 %copy-start.16 = (bf16[768,576]{1,0:T(8,128)(2,1)S(1)}, bf16[768,576]{1,0:T(8,128)(2,1)}, u32[]{:S(2)}) copy-start(bf16[768,576]{1,0:T(8,128)(2,1)} %copy-done.15) | copy-start | bytes 2654212
  393.0 124.3 %all-gather.18.cloned.1.call-start = ((), (), s32[]{:S(2)}) async-start(), calls=%async_computation.10 | async-start | bytes 2506752 | tf_op jit(solution)/shard_map/all_gather | solution.py:266
  397.8 75.2 %copy-start.7 = (bf16[1,128,768]{2,1,0:T(8,128)(2,1)S(1)}, bf16[1,128,768]{2,1,0:T(8,128)(2,1)}, u32[]{:S(2)}) copy-start(bf16[1,128,768]{2,1,0:T(8,128)(2,1)} %param.12) | copy-start | bytes 589828
  397.8 75.2 %copy-start.71 = (f32[128]{0:T(128)S(1)}, f32[128]{0:T(128)}, u32[]{:S(2)}) copy-start(f32[128]{0:T(128)} %get-tuple-element.156) | copy-start | bytes 1540
  457.9 58.5 %copy-start.11 = (f32[128,768]{1,0:T(8,128)S(1)}, f32[128,768]{1,0:T(8,128)}, u32[]{:S(2)}) copy-start(f32[128,768]{1,0:T(8,128)} %get-tuple-element.125) | copy-start | bytes 1179652
  457.9 58.4 %copy-start.75 = (f32[128]{0:T(128)S(1)}, f32[128]{0:T(128)}, u32[]{:S(2)}) copy-start(f32[128]{0:T(128)} %get-tuple-element.155) | copy-start | bytes 1540
  460.9 6.6 %collective-permute-start = (bf16[128,768]{1,0:T(8,128)(2,1)S(1)}, bf16[128,768]{1,0:T(8,128)(2,1)S(1)}, u32[]{:S(2)}, u32[]{:S(2)}) collective-permute-start(bf16[128,768]{1,0:T(8,128)(2,1)S(1)} %get-tuple-element.143), channel_id=1, source_target_pairs={{0,4},{4,8},{8,12},{12,0},{1,5},{5,9},{9,13},{13,1},{2,6},{6,10},{... | collective-permute-start | bytes 589832 | tf_op jit(solution)/shard_map/ppermute | solution.py:46
  461.0 8.1 %collective-permute-start.1 = (bf16[128,768]{1,0:T(8,128)(2,1)S(1)}, bf16[128,768]{1,0:T(8,128)(2,1)S(1)}, u32[]{:S(2)}, u32[]{:S(2)}) collective-permute-start(bf16[128,768]{1,0:T(8,128)(2,1)S(1)} %get-tuple-element.145), channel_id=1, source_target_pairs={{0,8},{4,12},{8,0},{12,4},{1,9},{5,13},{9,1},{13,5},{2,10},{6,14},... | collective-permute-start | bytes 589832 | tf_op jit(solution)/shard_map/ppermute | solution.py:46
  462.5 10.4 %collective-permute-start.2 = (bf16[128,768]{1,0:T(8,128)(2,1)S(1)}, bf16[128,768]{1,0:T(8,128)(2,1)S(1)}, u32[]{:S(2)}, u32[]{:S(2)}) collective-permute-start(bf16[128,768]{1,0:T(8,128)(2,1)S(1)} %get-tuple-element.144), channel_id=1, source_target_pairs={{0,12},{4,0},{8,4},{12,8},{1,13},{5,1},{9,5},{13,9},{2,14},{6,2},{... | collective-permute-start | bytes 589832 | tf_op jit(solution)/shard_map/ppermute | solution.py:46
  (61 other events, 306.5 us)
Sparse Core Ops, SparseCore 0:
  9.6 29.6 all-gather.9
  68.4 46.6 all-gather.11
  116.6 21.5 all-gather.13
  139.6 22.7 all-gather.15
  164.5 45.1 all-gather.19
  231.0 65.0 reduce-scatter.7
  299.9 65.1 reduce-scatter.5
  393.1 63.3 reduce-scatter.9
  458.9 42.8 all-gather.17
